TPU v7x, 32 devices: a whole 2x2x4 slice. The times are simulated.
32 devices in a mesh: groups: 2 (over y), tile: 16 (over z, x, core).
Axes of the slice: x: 2, y: 2, z: 4, core: 2. Of those that a mesh axis runs over, the one named last changes fastest.
Arguments:
- coarse: bfloat16 [12, 512, 512], P(None, ('groups', 'tile')), parts along dimension 1, may hold values from -6 to 6
- noise_field: bfloat16 [2, 12, 512, 512], P(None, None, ('groups', 'tile')), parts along dimension 2, may hold values from -6 to 6
- anchors: int32 [32, 2], P(('groups', 'tile')), parts along dimension 0, may hold values from 0 to 288
- counts: int32 [32], P(('groups', 'tile')), parts along dimension 0, may hold values from 1 to 2, as said below
- blend_weights: int32 [224, 224], replicated, may hold values from 1 to 16
- regress_lift: bfloat16 [12, 128], replicated, may hold values from -1.75 to 1.75
- regress_conv: bfloat16 [2, 9, 128, 128], replicated, may hold values from -0.1875 to 0.1875
- regress_head: bfloat16 [128, 12], replicated, may hold values from -0.5 to 0.5
- denoise_lift: bfloat16 [36, 128], replicated, may hold values from -1 to 1
- denoise_conv: bfloat16 [2, 9, 128, 128], replicated, may hold values from -0.1875 to 0.1875
- denoise_head: bfloat16 [128, 12], replicated, may hold values from -0.5 to 0.5
Outputs:
- ens_mean: float32 [12, 512, 512], P(None, ('groups', 'tile')), parts along dimension 1
- ens_var: float32 [12, 512, 512], P(None, ('groups', 'tile')), parts along dimension 1
There are 2 independent parts, one for each index of `groups`. A program takes and returns all parts, laid end to end along the dimension named above; an argument that names none is the same for every part. Nothing has to cross between parts.
Inputs may be any that keep to these rules, and one draw needn't show every extreme that they name: The first counts[s] slots of strip s are live; some strip has all 2 live in every draw.
All inputs are finite; a program needn't handle non-finite values.
Results may differ from a plain program's by a relative error of at most 0.0034.
Values may be sent and summed in bfloat16 or wider, within the bound.
A program may use at most 320 MiB of HBM per device.

v0:
```python
import math

import jax
import jax.numpy as jnp
from jax import lax
from jax.experimental import pallas as pl
from jax.experimental.pallas import tpu as pltpu
from jax.sharding import PartitionSpec as P

POOL = 4

skip_gain = 0.2
out_gain = 0.5 / math.sqrt(1.25)
in_gain = 1.0 / math.sqrt(1.25)


def exchange_kernel(moves, array_total, *refs):
    sources = refs[:array_total]
    targets = refs[array_total : 2 * array_total]
    send_sem, recv_sem = refs[2 * array_total :]
    mine = lax.axis_index("tile")
    count = lax.axis_size("tile")
    barrier = pltpu.get_barrier_semaphore()

    def holds(place):
        return jnp.logical_and(place >= 0, place < count)

    steps = sorted({move[3] for move in moves if move[3]})
    for step in steps:
        pl.semaphore_signal(
            barrier,
            inc=1,
            device_id={"tile": lax.rem(mine - step + count, count)},
            device_id_type=pl.DeviceIdType.MESH,
        )
    pl.semaphore_wait(barrier, len(steps))

    def copy_of(index):
        at, source, target, step = moves[index]
        return pltpu.make_async_remote_copy(
            src_ref=sources[at].at[source],
            dst_ref=targets[at].at[target],
            send_sem=send_sem.at[index],
            recv_sem=recv_sem.at[index],
            device_id={"tile": mine + step},
            device_id_type=pl.DeviceIdType.MESH,
        )

    for index, (at, source, target, step) in enumerate(moves):
        if step:

            @pl.when(holds(mine + step))
            def _():
                copy_of(index).start()

    for index, (at, source, target, step) in enumerate(moves):
        if step:

            @pl.when(jnp.logical_not(holds(mine - step)))
            def _():
                targets[at][target] = jnp.zeros(targets[at].shape[1:], targets[at].dtype)

        else:
            targets[at][target] = sources[at][source]
    for index, (at, source, target, step) in enumerate(moves):
        if step:

            @pl.when(holds(mine - step))
            def _():
                copy_of(index).wait_recv()

            @pl.when(holds(mine + step))
            def _():
                copy_of(index).wait_send()


def exchange(arrays, slots, moves, collective_id):
    vmem = pl.BlockSpec(memory_space=pltpu.VMEM)
    return pl.pallas_call(
        lambda *refs: exchange_kernel(moves, len(arrays), *refs),
        out_shape=tuple(
            jax.ShapeDtypeStruct((slot_count,) + array.shape[1:], array.dtype)
            for array, slot_count in zip(arrays, slots)
        ),
        in_specs=[vmem] * len(arrays),
        out_specs=(vmem,) * len(arrays),
        scratch_shapes=[
            pltpu.SemaphoreType.DMA((len(moves),)),
            pltpu.SemaphoreType.DMA((len(moves),)),
        ],
        compiler_params=pltpu.CompilerParams(collective_id=collective_id, has_side_effects=True),
        name="exchange%d" % collective_id,
    )(*arrays)


def conv(cells, kernel, row_pad):
    feat_in, feat_out = kernel.shape[1:]
    return lax.conv_general_dilated(
        cells,
        kernel.reshape(3, 3, feat_in, feat_out),
        (1, 1),
        ((row_pad, row_pad), (1, 1)),
        dimension_numbers=("NHWC", "HWIO", "NHWC"),
        preferred_element_type=jnp.float32,
    )


def residual_layer(hidden_act, conv_term):
    return (hidden_act.astype(jnp.float32) + jax.nn.silu(conv_term)).astype(jnp.bfloat16)


def regress(coarse, table, span, regress_lift, regress_conv, regress_head):
    channel_count, row_total, col_total = coarse.shape
    block_rows, block_cols = row_total // POOL, col_total // POOL
    layer_count = regress_conv.shape[0]
    owner = jnp.arange(col_total)[:, None] // POOL == jnp.arange(block_cols)[None, :]
    col_sums = jnp.dot(
        coarse.reshape(-1, col_total), owner.astype(jnp.bfloat16), preferred_element_type=jnp.float32
    )
    sums = col_sums.reshape(channel_count, block_rows, POOL, block_cols).sum(axis=2)
    coarse_low = (sums * (1.0 / (POOL * POOL))).astype(jnp.bfloat16)
    rows_first = coarse_low.transpose(1, 0, 2)
    rims = jnp.stack([rows_first[block_rows - layer_count :], rows_first[:layer_count]])
    moves = [(0, 0, at, at) for at in range(span - 1, -1, -1)] + [(1, 0, 0, 1), (1, 1, 1, -1)]
    tables, rims = exchange(
        (table[None], rims.reshape(2, layer_count * channel_count, block_cols)), (span, 2), moves, 0
    )
    rims = rims.reshape(2, layer_count, channel_count, block_cols)
    rimmed = jnp.concatenate([rims[0], rows_first, rims[1]]).transpose(1, 0, 2)
    hidden_act = jnp.einsum(
        "crw,ck->rwk", rimmed, regress_lift, preferred_element_type=jnp.float32
    ).astype(jnp.bfloat16)
    first_row = lax.axis_index("tile") * block_rows - layer_count
    domain_rows = lax.axis_size("tile") * block_rows
    for layer_index in range(layer_count):
        conv_term = conv(hidden_act[None], regress_conv[layer_index], 0)[0]
        hidden_act = residual_layer(hidden_act[1:-1], conv_term)
        first_row = first_row + 1
        rows = first_row + jnp.arange(hidden_act.shape[0])
        inside = jnp.logical_and(rows >= 0, rows < domain_rows)
        hidden_act = jnp.where(inside[:, None, None], hidden_act, jnp.zeros_like(hidden_act))
    reg_low = jnp.einsum(
        "rwk,kc->crw", hidden_act, regress_head, preferred_element_type=jnp.float32
    )
    wide = jnp.dot(
        reg_low.reshape(-1, block_cols),
        owner.T.astype(jnp.float32),
        precision=lax.Precision.HIGHEST,
        preferred_element_type=jnp.float32,
    ).reshape(channel_count, block_rows, 1, col_total)
    wide = jnp.broadcast_to(wide, (channel_count, block_rows, POOL, col_total))
    return coarse.astype(jnp.float32) + wide.reshape(coarse.shape), tables


def repeated(base, times):
    eye = jnp.eye(times, dtype=base.dtype)
    return (eye[:, None, :, None] * base[None, :, None, :]).reshape(
        times * base.shape[0], times * base.shape[1]
    )


def blend_kernel(slot_total, strip_rows, feat_rows, table_ref, heads_ref, weight_ref, acc_ref, den_ref):
    acc_ref[...] = jnp.zeros_like(acc_ref)
    den_ref[...] = jnp.zeros_like(den_ref)
    block_cols = heads_ref.shape[1]
    col_total = weight_ref.shape[1]

    def step(index, carry):
        offset = index // slot_total
        slot = index - offset * slot_total
        column = table_ref[offset * (slot_total + 1) + slot]
        live = slot < table_ref[offset * (slot_total + 1) + slot_total]

        @pl.when(live)
        def _():
            term = heads_ref[index]
            high = term.astype(jnp.bfloat16)
            low = (term - high.astype(jnp.float32)).astype(jnp.bfloat16)
            cols = lax.broadcasted_iota(jnp.int32, (block_cols, col_total), 1)
            blocks = lax.broadcasted_iota(jnp.int32, (block_cols, col_total), 0)
            pick = jnp.where(((cols - column) >> 2) == blocks, 1.0, 0.0).astype(jnp.bfloat16)
            dims = (((0,), (0,)), ((), ()))
            placed = lax.dot_general(
                high, pick, dims, preferred_element_type=jnp.float32
            ) + lax.dot_general(low, pick, dims, preferred_element_type=jnp.float32)
            start = pl.multiple_of(offset * strip_rows, strip_rows)
            weights = pltpu.roll(weight_ref[pl.ds(start, strip_rows), :], column, axis=1)
            den_ref[...] += weights
            for row in range(strip_rows):
                base = (row // POOL) * feat_rows
                acc_ref[row] += weights[row : row + 1, :] * placed[base : base + feat_rows, :]

        return carry

    lax.fori_loop(0, heads_ref.shape[0], step, 0)


def blend(table, heads, weights, slot_total, strip_rows, feat_rows):
    col_total = weights.shape[1]
    vmem = pl.BlockSpec(memory_space=pltpu.VMEM)
    return pl.pallas_call(
        lambda *refs: blend_kernel(slot_total, strip_rows, feat_rows, *refs),
        out_shape=(
            jax.ShapeDtypeStruct((strip_rows, feat_rows, col_total), jnp.float32),
            jax.ShapeDtypeStruct((strip_rows, col_total), jnp.float32),
        ),
        in_specs=[pl.BlockSpec(memory_space=pltpu.SMEM), vmem, vmem],
        out_specs=(vmem, vmem),
        name="blend",
    )(table, heads, weights)


def local(
    coarse,
    noise_field,
    anchors,
    counts,
    blend_weights,
    regress_lift,
    regress_conv,
    regress_head,
    denoise_lift,
    denoise_conv,
    denoise_head,
):
    members, channels, strip_rows, col_total = noise_field.shape
    patch_size = blend_weights.shape[0]
    width = denoise_lift.shape[1]
    span = patch_size // strip_rows
    slot_total = anchors.shape[1]
    block_rows = strip_rows // POOL
    block_cols = patch_size // POOL
    feat_rows = members * channels

    table = jnp.concatenate([anchors, counts[:, None]], axis=1)
    table = jnp.pad(table, ((0, 7), (0, 127 - slot_total)))
    reg_mean, tables = regress(coarse, table, span, regress_lift, regress_conv, regress_head)
    table = tables[:, 0, : slot_total + 1]

    fields = jnp.concatenate(
        [noise_field.reshape(feat_rows, strip_rows, col_total), reg_mean.astype(jnp.bfloat16), coarse]
    )
    field_count = fields.shape[0]
    row_sums = (
        fields.astype(jnp.float32)
        .reshape(field_count, block_rows, POOL, col_total)
        .sum(axis=2)
        .transpose(1, 0, 2)
    )
    row_sums = jnp.pad(row_sums, ((0, 0), (0, 0), (0, POOL - 1)))
    sums = sum(row_sums[:, :, at : at + col_total] for at in range(POOL))
    low_all = (sums * (1.0 / (POOL * POOL))).astype(jnp.bfloat16).reshape(-1, col_total)
    starts = table[:, :slot_total, None] + POOL * jnp.arange(block_cols, dtype=jnp.int32)
    pick = (starts.reshape(-1, 1) == jnp.arange(col_total, dtype=jnp.int32)[None]).astype(jnp.bfloat16)
    cut = lax.dot_general(
        pick, low_all, (((1,), (1,)), ((), ())), preferred_element_type=jnp.float32
    )
    cut = cut.astype(jnp.bfloat16).reshape(span, slot_total * block_cols, block_rows * field_count)
    farthest = range(span - 1, -1, -1)
    (low,) = exchange((cut,), (span,), [(0, at, at, -at) for at in farthest], 1)
    low = low.reshape(-1, block_rows * field_count)

    noise_base = repeated(denoise_lift[:channels], members)
    noise_base = jnp.pad(noise_base, ((0, 2 * channels), (0, 0)))
    cond_base = jnp.tile(denoise_lift[channels:], (1, members))
    cond_base = jnp.pad(cond_base, ((feat_rows, 0), (0, 0)))
    lifted = in_gain * jnp.dot(
        low, repeated(noise_base, block_rows), preferred_element_type=jnp.float32
    ) + jnp.dot(low, repeated(cond_base, block_rows), preferred_element_type=jnp.float32)
    hidden_act = (
        lifted.astype(jnp.bfloat16)
        .reshape(span, slot_total, block_cols, block_rows, members, width)
        .transpose(1, 4, 0, 3, 2, 5)
        .reshape(slot_total * members, span * block_rows, block_cols, width)
    )
    for layer_index in range(denoise_conv.shape[0]):
        hidden_act = residual_layer(hidden_act, conv(hidden_act, denoise_conv[layer_index], 1))
    hidden_act = (
        hidden_act.reshape(slot_total, members, span, block_rows, block_cols, width)
        .transpose(2, 0, 4, 3, 1, 5)
        .reshape(span * slot_total * block_cols, block_rows * members * width)
    )
    head = repeated(denoise_head, block_rows * members)
    head = jnp.pad(head, ((0, 0), (0, -head.shape[1] % 128)))
    heads = jnp.dot(hidden_act, head, preferred_element_type=jnp.float32)
    heads = heads.reshape(span, slot_total * block_cols, head.shape[1])
    (heads,) = exchange((heads,), (span,), [(0, at, at, at) for at in farthest], 2)

    weights = jnp.pad(blend_weights.astype(jnp.float32), ((0, 0), (0, col_total - patch_size)))
    acc, denom = blend(
        table.reshape(-1),
        heads.reshape(span * slot_total, block_cols, head.shape[1]),
        weights,
        slot_total,
        strip_rows,
        feat_rows,
    )
    acc = acc.reshape(strip_rows, members, channels, col_total).transpose(1, 2, 0, 3)
    numer = skip_gain * noise_field.astype(jnp.float32) * denom + out_gain * acc
    outs = reg_mean[None] + numer / jnp.maximum(denom, 1.0)
    ens_mean = jnp.mean(outs, axis=0)
    ens_var = jnp.mean((outs - ens_mean[None]) ** 2, axis=0)
    return (ens_mean, ens_var)


def solution(mesh):
    in_specs = (
        P(None, ("groups", "tile"), None),
        P(None, None, ("groups", "tile"), None),
        P(("groups", "tile"), None),
        P(("groups", "tile")),
        P(),
        P(),
        P(),
        P(),
        P(),
        P(),
        P(),
    )
    out_specs = (P(None, ("groups", "tile"), None), P(None, ("groups", "tile"), None))
    return jax.shard_map(local, mesh=mesh, in_specs=in_specs, out_specs=out_specs, check_vma=False)
```

profile of v0, /device:TPU:17, one launch (start us, length us, event | category | flops | bytes accessed | tf_op | source)
XLA Modules:
  0.0 140.7 jit_solution(4983841705052462110)
XLA Ops:
  1.3 0.7 pad_add_fusion
  2.0 0.6 pad_bitcast_fusion.refs_0_
  2.7 1.2 fusion.24
  4.0 0.6 pad_maximum_fusion.refs_1_
  4.6 8.4 %exchange0.1 = (s32[14,8,128]{2,1,0:T(8,128)}, bf16[2,24,128]{2,1,0:T(8,128)(2,1)}) custom-call(s32[1,8,128]{2,1,0:T(8,128)} %pad_bitcast_fusion.refs_0_, bf16[2,24,128]{2,1,0:T(8,128)(2,1)} %pad_maximum_fusion.refs_1_), custom_call_target="tpu_custom_call" | custom-call | tf_op jit(solution)/shard_map/exchange0/pallas_call | solution.py:79
  13.0 0.8 fusion.67
  13.9 0.6 reshape_squeeze.17.refs_0_
  14.5 1.0 concatenate.21
  15.5 1.1 fusion.66
  16.6 0.7 fusion.69
  17.4 0.3 convolution_convert_fusion
  17.6 0.2 copy.62
  17.9 1.4 convolution_select_fusion
  19.5 0.1 broadcast_select_fusion
  19.9 0.5 convolution_select_fusion.1
  20.5 0.2 convolution_bitcast_fusion
  20.7 0.4 fusion.25
  21.3 0.1 reshape.232
  21.4 0.8 fusion.64
  22.3 0.1 concatenate.19
  22.4 1.2 convert_reduce_fusion
  23.6 0.7 fusion.13
  24.4 0.1 copy.54
  24.7 1.0 fusion.5
  25.7 1.2 copy.56
  26.8 23.8 %exchange1.1 = bf16[14,112,192]{2,1,0:T(8,128)(2,1)} custom-call(bf16[14,112,192]{2,1,0:T(8,128)(2,1)} %bitcast.118), custom_call_target="tpu_custom_call" | custom-call | tf_op jit(solution)/shard_map/exchange1/pallas_call | solution.py:79
  50.9 0.4 broadcast_multiply_fusion.3
  51.3 2.2 %fusion.70 = f32[1568,1024]{1,0:T(8,128)S(1)} fusion(bf16[1568,192]{1,0:T(8,128)(2,1)} %bitcast.111, bf16[192,1024]{1,0:T(8,128)(2,1)S(1)} %bitcast.121), kind=kOutput, calls=%fused_computation.119 | convolution fusion | flops 616562688 | bytes 7417856 | tf_op jit(solution)/shard_map/dot_general | solution.py:267
  53.6 1.0 add_convert_fusion
  54.6 3.5 %reshape.236 = bf16[14,2,56,4,2,128]{5,4,3,2,1,0:T(2,128)(2,1)} reshape(bf16[1568,1024]{1,0:T(8,128)(2,1)S(1)} %add_convert_fusion) | data formatting | bytes 6422528 | tf_op jit(solution)/shard_map/reshape | solution.py:272
  58.1 4.6 %copy.57 = bf16[2,2,14,4,56,128]{5,1,0,4,3,2:T(2,128)(2,1)S(1)} copy(bf16[2,2,14,4,56,128]{5,1,3,4,0,2:T(2,128)(2,1)} %bitcast.110) | data formatting | bytes 6422528 | tf_op jit(solution)/shard_map/transpose | solution.py:273
  62.8 11.2 %fusion.3 = bf16[4,56,56,128]{3,0,2,1:T(4,128)(2,1)S(1)} fusion(bf16[4,56,56,128]{3,0,2,1:T(4,128)(2,1)S(1)} %bitcast.115, bf16[3,3,128,128]{3,2,1,0:T(8,128)(2,1)S(1)} %bitcast.135), kind=kOutput, calls=%fused_computation.6 | convolution fusion | flops 3623059456 | bytes 6717440 | tf_op jit(solution)/shard_map/conv_general_dilated | solution.py:98
  74.1 11.4 %fusion.2 = bf16[4,56,56,128]{3,0,2,1:T(4,128)(2,1)S(1)} fusion(bf16[4,56,56,128]{3,0,2,1:T(4,128)(2,1)S(1)} %fusion.3, bf16[3,3,128,128]{3,2,1,0:T(8,128)(2,1)S(1)} %bitcast.134), kind=kOutput, calls=%fused_computation.5 | convolution fusion | flops 3623059456 | bytes 6717440 | tf_op jit(solution)/shard_map/conv_general_dilated | solution.py:98
  85.5 4.9 %copy.58 = bf16[14,2,56,4,2,128]{5,4,3,2,1,0:T(2,128)(2,1)} copy(bf16[14,2,56,4,2,128]{5,4,1,2,3,0:T(2,128)(2,1)S(1)} %bitcast.116) | data formatting | bytes 6422528 | tf_op jit(solution)/shard_map/transpose | solution.py:280
  90.3 7.0 %dot_general.39 = bf16[14,112,1024]{2,1,0:T(8,128)(2,1)S(1)} reshape(bf16[14,2,56,4,2,128]{5,4,3,2,1,0:T(2,128)(2,1)} %copy.58) | data formatting | bytes 6422528 | tf_op jit(solution)/shard_map/dot_general | solution.py:285
  97.4 0.7 copy.82
  98.1 1.1 copy.59
  99.2 1.9 %fusion.20.refs_0_ = f32[14,112,128]{2,1,0:T(8,128)} fusion(bf16[14,112,1024]{2,1,0:T(8,128)(2,1)S(1)} %dot_general.39, bf16[1024,96]{1,0:T(8,128)(2,1)S(1)} %copy.59), kind=kOutput, calls=%fused_computation.40 | convolution fusion | flops 411041792 | bytes 4210688 | tf_op jit(solution)/shard_map/dot_general | solution.py:285
  101.2 26.0 %exchange2.1 = f32[14,112,128]{2,1,0:T(8,128)} custom-call(f32[14,112,128]{2,1,0:T(8,128)} %fusion.20.refs_0_), custom_call_target="tpu_custom_call" | custom-call | tf_op jit(solution)/shard_map/exchange2/pallas_call | solution.py:79
  127.2 1.0 convert_element_type.117
  128.1 0.8 pad.29.refs_2_
  129.0 7.9 %blend.1 = (f32[16,24,512]{2,1,0:T(8,128)}, f32[16,512]{1,0:T(8,128)}) custom-call(s32[42]{0:T(128)} %reshape_squeeze.17.refs_0_, f32[28,56,128]{2,1,0:T(8,128)} %bitcast.117, f32[224,512]{1,0:T(8,128)} %pad.29.refs_2_), custom_call_target="tpu_custom_call" | custom-call | tf_op jit(solution)/shard_map/blend/pallas_call | solution.py:201
  136.9 0.8 broadcast_multiply_fusion.6
  137.7 1.2 broadcast_multiply_fusion
  138.9 0.5 copy.60
  139.4 0.2 fusion.63
  139.6 0.3 multiply_reduce_fusion
  139.9 0.8 broadcast_multiply_fusion.1
  (71 shorter events, 1.6 us)
Async XLA Ops:
  0.6 16.7 %copy-start = (bf16[12,128]{1,0:T(8,128)(2,1)S(1)}, bf16[12,128]{1,0:T(8,128)(2,1)}, u32[]{:S(2)}) copy-start(bf16[12,128]{1,0:T(8,128)(2,1)} %param.16) | copy-start | bytes 9220
  0.6 19.2 %copy-start.11 = (pred[8,17]{0,1:T(8,128)(4,1)S(1)}, pred[8,17]{0,1:T(8,128)(4,1)}, u32[]{:S(2)}) copy-start(pred[8,17]{0,1:T(8,128)(4,1)} %constant.89) | copy-start | bytes 412
  3.9 16.6 %copy-start.10 = (bf16[128,12]{0,1:T(8,128)(2,1)S(1)}, bf16[128,12]{0,1:T(8,128)(2,1)}, u32[]{:S(2)}) copy-start(bf16[128,12]{0,1:T(8,128)(2,1)} %param.18) | copy-start | bytes 9220
  17.8 3.6 %copy-start.5 = (bf16[12,16,512]{2,1,0:T(8,128)(2,1)S(1)}, bf16[12,16,512]{2,1,0:T(8,128)(2,1)}, u32[]{:S(2)}) copy-start(bf16[12,16,512]{2,1,0:T(8,128)(2,1)} %param.11) | copy-start | bytes 589828
  17.9 4.4 %copy-start.2 = (bf16[2,12,16,512]{3,2,1,0:T(8,128)(2,1)S(1)}, bf16[2,12,16,512]{3,2,1,0:T(8,128)(2,1)}, u32[]{:S(2)}) copy-start(bf16[2,12,16,512]{3,2,1,0:T(8,128)(2,1)} %param.12) | copy-start | bytes 1179652
  20.5 30.2 %copy-start.8 = (bf16[36,128]{1,0:T(8,128)(2,1)S(1)}, bf16[36,128]{1,0:T(8,128)(2,1)}, u32[]{:S(2)}) copy-start(bf16[36,128]{1,0:T(8,128)(2,1)} %param.19) | copy-start | bytes 27652
  20.5 30.2 %slice-start = ((bf16[36,128]{1,0:T(8,128)(2,1)}), bf16[12,128]{1,0:T(8,128)(2,1)S(1)}, s32[]{:S(2)}) async-start(bf16[36,128]{1,0:T(8,128)(2,1)} %param.19), calls=%async_computation | async-start | bytes 8192 | tf_op jit(solution)/shard_map/slice | solution.py:263
  51.2 2.3 %copy-start.1 = (bf16[14,112,192]{2,1,0:T(8,128)(2,1)S(1)}, bf16[14,112,192]{2,1,0:T(8,128)(2,1)}, u32[]{:S(2)}) copy-start(bf16[14,112,192]{2,1,0:T(8,128)(2,1)} %exchange1.1) | copy-start | bytes 1806340
  58.1 4.6 %copy-start.7 = (bf16[2,9,128,128]{3,2,1,0:T(8,128)(2,1)S(1)}, bf16[2,9,128,128]{3,2,1,0:T(8,128)(2,1)}, u32[]{:S(2)}) copy-start(bf16[2,9,128,128]{3,2,1,0:T(8,128)(2,1)} %param.20) | copy-start | bytes 1769476
  85.4 11.9 %copy-start.9 = (bf16[128,12]{0,1:T(8,128)(2,1)S(1)}, bf16[128,12]{0,1:T(8,128)(2,1)}, u32[]{:S(2)}) copy-start(bf16[128,12]{0,1:T(8,128)(2,1)} %param.21) | copy-start | bytes 9220
  101.2 38.2 %copy-start.3 = (bf16[2,12,16,512]{3,2,1,0:T(8,128)(2,1)S(1)}, bf16[2,12,16,512]{3,2,1,0:T(8,128)(2,1)}, u32[]{:S(2)}) copy-start(bf16[2,12,16,512]{3,2,1,0:T(8,128)(2,1)} %param.12) | copy-start | bytes 1179652
  101.2 38.2 %copy-start.4 = (f32[12,16,512]{2,1,0:T(8,128)S(1)}, f32[12,16,512]{2,1,0:T(8,128)}, u32[]{:S(2)}) copy-start(f32[12,16,512]{2,1,0:T(8,128)} %get-tuple-element.11) | copy-start | bytes 1179652
  139.6 1.1 copy-start.6
where the time goes:
time: 141 us
  Pallas kernels  66.1 us (47%)
  matrix products  32.7 us (23%)
  local copies, waits for them, and re-layouts  30.8 us (22%)
  other arithmetic  9.08 us (6%)
  between operations  1.95 us (1%)
    pallas_call x3, Pallas kernels, exchange(): pl.pallas_call(lambda *refs: exchange_kernel(moves, len(arrays), *refs),...  58.2 us
    conv_general_dilated x4, matrix products, conv(): lax.conv_general_dilated(cells, kernel.reshape(3, 3, feat_in, feat_out),...  24.5 us
    pallas_call x1, Pallas kernels, blend(): pl.pallas_call(lambda *refs: blend_kernel(slot_total, strip_rows, feat_ro...  7.92 us
    dot_general x1, local copies, waits for them, and re-layouts, local(): heads = jnp.dot(hidden_act, head, preferred_element_type=jnp.float32)  6.98 us
    transpose x1, local copies, waits for them, and re-layouts, local(): hidden_act = hidden_act.reshape(slot_total, members, span, block_rows, bl...  4.86 us
    transpose x1, local copies, waits for them, and re-layouts, local(): hidden_act = lifted.astype(jnp.bfloat16).reshape(span, slot_total, block_...  4.62 us
    reshape x1, local copies, waits for them, and re-layouts, local(): hidden_act = lifted.astype(jnp.bfloat16).reshape(span, slot_total, block_...  3.54 us

commit v1 on v0

--- a/solution.py
+++ b/solution.py
@@ -257,7 +257,14 @@
     )
     cut = cut.astype(jnp.bfloat16).reshape(span, slot_total * block_cols, block_rows * field_count)
     farthest = range(span - 1, -1, -1)
+    half = slot_total * block_cols // 2
+    tail = jnp.concatenate([cut[:, :half, 128:], cut[:, half:, 128:]], axis=2)
+    cut = jnp.concatenate([cut[:, :, :128], tail], axis=1)
     (low,) = exchange((cut,), (span,), [(0, at, at, -at) for at in farthest], 1)
+    side = (cut.shape[2] // 2) if half else 0
+    tail = low[:, 2 * half :]
+    tail = jnp.concatenate([tail[:, :, :side], tail[:, :, side:]], axis=1)
+    low = jnp.concatenate([low[:, : 2 * half], tail], axis=2)
     low = low.reshape(-1, block_rows * field_count)
 
     noise_base = repeated(denoise_lift[:channels], members)
@@ -281,10 +288,21 @@
         .reshape(span * slot_total * block_cols, block_rows * members * width)
     )
     head = repeated(denoise_head, block_rows * members)
-    head = jnp.pad(head, ((0, 0), (0, -head.shape[1] % 128)))
+    head_lanes = head.shape[1]
+    spare = -head_lanes % 128
+    head = jnp.pad(head, ((0, 0), (0, spare)))
     heads = jnp.dot(hidden_act, head, preferred_element_type=jnp.float32)
     heads = heads.reshape(span, slot_total * block_cols, head.shape[1])
+    chunks = head_lanes // spare
+    lot = heads.shape[1] // (chunks + 1)
+    last = heads[:, chunks * lot :]
+    side = jnp.concatenate([last[:, :, at * spare : (at + 1) * spare] for at in range(chunks)], axis=1)
+    heads = jnp.concatenate([heads[:, : chunks * lot, :head_lanes], side], axis=2)
     (heads,) = exchange((heads,), (span,), [(0, at, at, at) for at in farthest], 2)
+    last = [heads[:, at * lot : (at + 1) * lot, head_lanes:] for at in range(chunks)]
+    last = jnp.concatenate(last, axis=2)
+    heads = jnp.concatenate([heads[:, :, :head_lanes], last], axis=1)
+    heads = jnp.pad(heads, ((0, 0), (0, 0), (0, spare)))
 
     weights = jnp.pad(blend_weights.astype(jnp.float32), ((0, 0), (0, col_total - patch_size)))
     acc, denom = blend(

time: 141 us -> 135 us (0.957)
  Pallas kernels: 66.1 us -> 55.7 us
  other arithmetic: 9.08 us -> 12.6 us
  local copies, waits for them, and re-layouts: 30.8 us -> 34.1 us
  matrix products: 32.7 us -> 29.8 us
    pallas_call x3, Pallas kernels: 58.2 us -> 48 us  [exchange(): pl.pallas_call(lambda *refs: exchange_kernel(moves, len(arrays), *refs),...]
    concatenate x0 -> x4, other arithmetic: none -> 4.43 us  [the longest x1 2.2 us: local(): heads = jnp.concatenate([heads[:, :, :head_lanes], last], axis=1)]
    slice x0 -> x7, local copies, waits for them, and re-layouts: none -> 4 us  [the longest x1 1.44 us: local(): heads[:, at * lot:(at + 1) * lot, head_lanes:]]
where the time goes in v1:
time: 135 us; the launch traced here: 134 us
  Pallas kernels  55.7 us (41%)
  local copies, waits for them, and re-layouts  34.1 us (25%)
  matrix products  29.8 us (22%)
  other arithmetic  12.6 us (9%)
  between operations  1.99 us (1%)
    pallas_call x3, Pallas kernels, exchange(): pl.pallas_call(lambda *refs: exchange_kernel(moves, len(arrays), *refs),...  48 us
    conv_general_dilated x4, matrix products, conv(): lax.conv_general_dilated(cells, kernel.reshape(3, 3, feat_in, feat_out),...  23.8 us
    pallas_call x1, Pallas kernels, blend(): pl.pallas_call(lambda *refs: blend_kernel(slot_total, strip_rows, feat_ro...  7.65 us
    dot_general x1, local copies, waits for them, and re-layouts, local(): heads = jnp.dot(hidden_act, head, preferred_element_type=jnp.float32)  7 us
    transpose x1, local copies, waits for them, and re-layouts, local(): hidden_act = hidden_act.reshape(slot_total, members, span, block_rows, bl...  4.88 us
    transpose x1, local copies, waits for them, and re-layouts, local(): hidden_act = lifted.astype(jnp.bfloat16).reshape(span, slot_total, block_...  4.62 us
    reshape x1, local copies, waits for them, and re-layouts, local(): hidden_act = lifted.astype(jnp.bfloat16).reshape(span, slot_total, block_...  3.55 us

profile of v1, /device:TPU:17, one launch (start us, length us, event | category | flops | bytes accessed | tf_op | source)
XLA Modules:
  0.0 134.1 jit_solution(16851713748622380172)
XLA Ops:
  1.3 0.7 pad_add_fusion
  2.0 0.6 pad_bitcast_fusion.refs_0_
  2.7 1.2 fusion.29
  4.0 0.6 pad_maximum_fusion.refs_1_
  4.6 8.4 %exchange0.1 = (s32[14,8,128]{2,1,0:T(8,128)}, bf16[2,24,128]{2,1,0:T(8,128)(2,1)}) custom-call(s32[1,8,128]{2,1,0:T(8,128)} %pad_bitcast_fusion.refs_0_, bf16[2,24,128]{2,1,0:T(8,128)(2,1)} %pad_maximum_fusion.refs_1_), custom_call_target="tpu_custom_call" | custom-call | tf_op jit(solution)/shard_map/exchange0/pallas_call | solution.py:79
  13.0 0.8 fusion.76
  13.9 0.7 reshape_squeeze.17.refs_0_
  14.5 1.0 concatenate.45
  15.5 1.1 fusion.75
  16.7 0.7 fusion.78
  17.4 0.3 convolution_convert_fusion
  18.0 0.7 convolution_select_fusion
  19.2 0.5 convolution_select_fusion.1
  19.8 0.2 convolution_bitcast_fusion
  20.0 0.4 fusion.30
  20.7 0.8 fusion.69
  21.7 1.2 convert_reduce_fusion
  22.9 0.7 fusion.18
  24.0 0.9 fusion.5
  24.9 0.3 copy.78
  25.4 1.0 maximum_maximum_fusion.2.refs_0_
  26.4 18.8 %exchange1.1 = bf16[14,168,128]{2,1,0:T(8,128)(2,1)} custom-call(bf16[14,168,128]{2,1,0:T(8,128)(2,1)} %maximum_maximum_fusion.2.refs_0_), custom_call_target="tpu_custom_call" | custom-call | tf_op jit(solution)/shard_map/exchange1/pallas_call | solution.py:79
  45.1 1.2 fusion.73
  46.3 1.0 slice.119
  47.7 0.4 broadcast_multiply_fusion.3
  48.2 1.0 fusion.79
  49.2 1.0 add_convert_fusion
  50.2 3.6 %reshape.236 = bf16[14,2,56,4,2,128]{5,4,3,2,1,0:T(2,128)(2,1)} reshape(bf16[1568,1024]{1,0:T(8,128)(2,1)S(1)} %add_convert_fusion) | data formatting | bytes 6422528 | tf_op jit(solution)/shard_map/reshape | solution.py:279
  53.8 4.6 %copy.79 = bf16[2,2,14,4,56,128]{5,1,0,4,3,2:T(2,128)(2,1)S(1)} copy(bf16[2,2,14,4,56,128]{5,1,3,4,0,2:T(2,128)(2,1)} %bitcast.111) | data formatting | bytes 6422528 | tf_op jit(solution)/shard_map/transpose | solution.py:280
  58.5 11.2 %fusion.3 = bf16[4,56,56,128]{3,0,2,1:T(4,128)(2,1)S(1)} fusion(bf16[4,56,56,128]{3,0,2,1:T(4,128)(2,1)S(1)} %bitcast.117, bf16[3,3,128,128]{3,2,1,0:T(8,128)(2,1)S(1)} %bitcast.138), kind=kOutput, calls=%fused_computation.6 | convolution fusion | flops 3623059456 | bytes 6717440 | tf_op jit(solution)/shard_map/conv_general_dilated | solution.py:98
  69.7 11.4 %fusion.2 = bf16[4,56,56,128]{3,0,2,1:T(4,128)(2,1)S(1)} fusion(bf16[4,56,56,128]{3,0,2,1:T(4,128)(2,1)S(1)} %fusion.3, bf16[3,3,128,128]{3,2,1,0:T(8,128)(2,1)S(1)} %bitcast.137), kind=kOutput, calls=%fused_computation.5 | convolution fusion | flops 3623059456 | bytes 6717440 | tf_op jit(solution)/shard_map/conv_general_dilated | solution.py:98
  81.1 4.9 %copy.80 = bf16[14,2,56,4,2,128]{5,4,3,2,1,0:T(2,128)(2,1)} copy(bf16[14,2,56,4,2,128]{5,4,1,2,3,0:T(2,128)(2,1)S(1)} %bitcast.118) | data formatting | bytes 6422528 | tf_op jit(solution)/shard_map/transpose | solution.py:287
  86.0 7.0 %dot_general.39 = bf16[14,112,1024]{2,1,0:T(8,128)(2,1)S(1)} reshape(bf16[14,2,56,4,2,128]{5,4,3,2,1,0:T(2,128)(2,1)} %copy.80) | data formatting | bytes 6422528 | tf_op jit(solution)/shard_map/dot_general | solution.py:294
  93.1 0.7 copy.104
  93.8 1.1 copy.81
  94.9 1.0 fusion.25
  96.2 1.1 maximum_maximum_fusion.1.refs_0_
  97.3 20.9 %exchange2.1 = f32[14,84,128]{2,1,0:T(8,128)} custom-call(f32[14,84,128]{2,1,0:T(8,128)} %maximum_maximum_fusion.1.refs_0_), custom_call_target="tpu_custom_call" | custom-call | tf_op jit(solution)/shard_map/exchange2/pallas_call | solution.py:79
  118.2 1.4 %fusion.72 = (f32[14,28,32]{2,1,0:T(8,128)S(1)}, f32[14,28,32]{2,1,0:T(8,128)S(1)}, f32[14,28,32]{2,1,0:T(8,128)S(1)}) fusion(f32[14,84,128]{2,1,0:T(8,128)} %exchange2.1), kind=kLoop, calls=%fused_computation.126 | loop fusion | bytes 301056 | tf_op jit(solution)/shard_map/slice | solution.py:302
  119.6 2.2 %select_maximum_fusion = f32[14,112,128]{2,1,0:T(8,128)} fusion(f32[14,84,96]{2,1,0:T(8,128)} %bitcast.116, f32[14,28,32]{2,1,0:T(8,128)S(1)} %get-tuple-element.18, f32[14,28,32]{2,1,0:T(8,128)S(1)} %get-tuple-element.19, f32[14,28,32]{2,1,0:T(8,128)S(1)} %get-tuple-element.17), kind=kLoop, calls=%fused_computation.16 | loop fusion | flops 1605632 | bytes 1404928 | tf_op jit(solution)/shard_map/concatenate | solution.py:304
  121.8 0.8 pad.34.refs_2_
  122.7 7.7 %blend.1 = (f32[16,24,512]{2,1,0:T(8,128)}, f32[16,512]{1,0:T(8,128)}) custom-call(s32[42]{0:T(128)} %reshape_squeeze.17.refs_0_, f32[28,56,128]{2,1,0:T(8,128)} %bitcast.121, f32[224,512]{1,0:T(8,128)} %pad.34.refs_2_), custom_call_target="tpu_custom_call" | custom-call | tf_op jit(solution)/shard_map/blend/pallas_call | solution.py:201
  130.3 0.8 broadcast_multiply_fusion.6
  131.1 1.2 broadcast_multiply_fusion
  132.3 0.5 copy.82
  132.8 0.2 fusion.68
  133.1 0.3 multiply_reduce_fusion
  133.3 0.8 broadcast_multiply_fusion.1
  (82 shorter events, 2.8 us)
Async XLA Ops:
  0.6 16.8 %copy-start = (bf16[12,128]{1,0:T(8,128)(2,1)S(1)}, bf16[12,128]{1,0:T(8,128)(2,1)}, u32[]{:S(2)}) copy-start(bf16[12,128]{1,0:T(8,128)(2,1)} %param.16) | copy-start | bytes 9220
  0.6 17.3 %copy-start.11 = (pred[8,17]{0,1:T(8,128)(4,1)S(1)}, pred[8,17]{0,1:T(8,128)(4,1)}, u32[]{:S(2)}) copy-start(pred[8,17]{0,1:T(8,128)(4,1)} %constant.91) | copy-start | bytes 412
  18.6 1.2 copy-start.10
  19.1 1.6 %copy-start.4 = (bf16[12,16,512]{2,1,0:T(8,128)(2,1)S(1)}, bf16[12,16,512]{2,1,0:T(8,128)(2,1)}, u32[]{:S(2)}) copy-start(bf16[12,16,512]{2,1,0:T(8,128)(2,1)} %param.11) | copy-start | bytes 589828
  19.7 1.9 %copy-start.1 = (bf16[2,12,16,512]{3,2,1,0:T(8,128)(2,1)S(1)}, bf16[2,12,16,512]{3,2,1,0:T(8,128)(2,1)}, u32[]{:S(2)}) copy-start(bf16[2,12,16,512]{3,2,1,0:T(8,128)(2,1)} %param.12) | copy-start | bytes 1179652
  25.3 22.2 %copy-start.8 = (bf16[36,128]{1,0:T(8,128)(2,1)S(1)}, bf16[36,128]{1,0:T(8,128)(2,1)}, u32[]{:S(2)}) copy-start(bf16[36,128]{1,0:T(8,128)(2,1)} %param.19) | copy-start | bytes 27652
  25.3 22.3 %slice-start = ((bf16[36,128]{1,0:T(8,128)(2,1)}), bf16[12,128]{1,0:T(8,128)(2,1)S(1)}, s32[]{:S(2)}) async-start(bf16[36,128]{1,0:T(8,128)(2,1)} %param.19), calls=%async_computation | async-start | bytes 8192 | tf_op jit(solution)/shard_map/slice | solution.py:270
  53.8 4.6 %copy-start.6 = (bf16[2,9,128,128]{3,2,1,0:T(8,128)(2,1)S(1)}, bf16[2,9,128,128]{3,2,1,0:T(8,128)(2,1)}, u32[]{:S(2)}) copy-start(bf16[2,9,128,128]{3,2,1,0:T(8,128)(2,1)} %param.20) | copy-start | bytes 1769476
  86.0 7.0 %copy-start.9 = (bf16[128,12]{0,1:T(8,128)(2,1)S(1)}, bf16[128,12]{0,1:T(8,128)(2,1)}, u32[]{:S(2)}) copy-start(bf16[128,12]{0,1:T(8,128)(2,1)} %param.21) | copy-start | bytes 9220
  96.2 25.7 %copy-start.7 = (s32[224,224]{1,0:T(8,128)S(1)}, s32[224,224]{1,0:T(8,128)}, u32[]{:S(2)}) copy-start(s32[224,224]{1,0:T(8,128)} %param.15) | copy-start | bytes 602116
  121.8 11.0 %copy-start.2 = (bf16[2,12,16,512]{3,2,1,0:T(8,128)(2,1)S(1)}, bf16[2,12,16,512]{3,2,1,0:T(8,128)(2,1)}, u32[]{:S(2)}) copy-start(bf16[2,12,16,512]{3,2,1,0:T(8,128)(2,1)} %param.12) | copy-start | bytes 1179652
  121.8 11.0 %copy-start.3 = (f32[12,16,512]{2,1,0:T(8,128)S(1)}, f32[12,16,512]{2,1,0:T(8,128)}, u32[]{:S(2)}) copy-start(f32[12,16,512]{2,1,0:T(8,128)} %get-tuple-element.11) | copy-start | bytes 1179652
  133.1 1.1 copy-start.5
